TPU v7x, 512 devices: a whole 4x4x16 slice. The times are simulated.
512 devices in a mesh: row: 32 (over z, core), col: 16 (over x, y).
Axes of the slice: x: 4, y: 4, z: 16, core: 2. Of those that a mesh axis runs over, the one named last changes fastest.
Arguments:
- trailing: float32 [16384, 16384], P('row', 'col'), may hold values from -6 to 6
- panel: float32 [16384, 512], P(('row', 'col')), may hold values from -0.25 to 0.25
- inv_factor: float32 [512, 512], P(None, 'col'), as said below
- later_series: float32 [16384, 1024], P('row', 'col'), may hold values from -6 to 6
- fold_series: float32 [512, 1024], P('row', 'col'), may hold values from -6 to 6
- fold_len: int32 [1024], P('col'), may hold values from 1 to 32, as said below
Outputs:
- new_trailing: float32 [16384, 16384], P('row', 'col')
- new_series: float32 [16384, 1024], P('row', 'col')
Inputs may be any that keep to these rules, and one draw needn't show every extreme that they name: inv_factor is lower triangular with a diagonal between 1 and 2. `fold_len`: some series reach all 32 blocks and some only one.
All inputs are finite; a program needn't handle non-finite values.
Results may differ from a plain program's by a relative error of at most 0.0003.
Values sent between devices are 32-bit elements; how exact they have to be, the bound alone decides.
No kernel may reach another device: no remote copies, remote signals or barrier semaphores. Data moves between devices by JAX's collectives and lax.ppermute only.
A program may use at most 64 MiB of HBM per device.

v0:
```python
import jax
import jax.numpy as jnp
from jax import lax
from jax.sharding import PartitionSpec as P


def spread(array, axis, root):
    mine = lax.axis_index(axis) == root
    return lax.psum(jnp.where(mine, array, jnp.zeros_like(array)), axis)


def on_device(trailing, panel, inv_factor, later_series, fold_series, fold_len):
    highest = lax.Precision.HIGHEST
    contract = (((1,), (1,)), ((), ()))
    inverse = lax.all_gather(inv_factor, "col", axis=1, tiled=True)
    solved_mine = lax.dot_general(
        panel, inverse, contract, precision=highest, preferred_element_type=jnp.float32
    )
    row_block = lax.all_gather(solved_mine, "col", axis=0, tiled=True)
    rows_here = trailing.shape[0]
    cols_here = trailing.shape[1]
    tiles_across = cols_here // rows_here
    row_pos = lax.axis_index("row")
    col_pos = lax.axis_index("col")
    pieces = []
    for offset in range(tiles_across):
        source = col_pos * tiles_across + offset
        pieces.append(spread(row_block, "row", source))
    col_panel = jnp.concatenate(pieces, 0)
    update = lax.dot_general(
        row_block, col_panel, contract, precision=highest, preferred_element_type=jnp.float32
    )
    col_tile = (col_pos * cols_here + jnp.arange(cols_here, dtype=jnp.int32)) // rows_here
    lower = col_tile <= row_pos
    new_trailing = jnp.where(lower[None, :], trailing - update, trailing)
    fold_all = lax.all_gather(fold_series, "row", axis=0, tiled=True)
    innovations = jnp.dot(inverse, fold_all, precision=highest, preferred_element_type=jnp.float32)
    correction = jnp.dot(
        row_block, innovations, precision=highest, preferred_element_type=jnp.float32
    )
    active = row_pos < fold_len
    new_series = jnp.where(active[None, :], later_series - correction, later_series)
    return (new_trailing, new_series)


def solution(mesh):
    in_specs = (
        P("row", "col"),
        P(("row", "col"), None),
        P(None, "col"),
        P("row", "col"),
        P("row", "col"),
        P("col"),
    )
    out_specs = (P("row", "col"), P("row", "col"))
    return jax.shard_map(
        on_device, mesh=mesh, in_specs=in_specs, out_specs=out_specs, check_vma=False
    )
```

profile of v0, /device:TPU:1, one launch (start us, length us, event | category | flops | bytes accessed | tf_op | source)
XLA Modules:
  0.0 367.0 jit_solution(11055402713785752273)
XLA Ops:
  7.2 0.0 copy-start
  7.2 0.0 all-gather.3.cloned.1.call-start
  7.2 0.7 all-gather.3.cloned.1.call-update
  7.9 0.0 all-gather.5.cloned.1.call-start
  8.0 64.4 %all-gather.3.cloned.1.call-done = f32[512,512]{0,1:T(8,128)} async-done(((f32[512,32]{0,1:T(8,128)}), f32[512,512]{0,1:T(8,128)}) %all-gather.3.cloned.1.call-update) | async-done | bytes 1048592 | tf_op jit(solution)/shard_map/all_gather | solution.py:15
  72.3 0.0 copy-done
  72.3 2.6 fusion.12
  74.9 0.0 all-gather.5.cloned.1.call-update
  74.9 0.0 all-reduce.3.cloned.1.call-start
  75.0 0.0 copy-start.4
  75.0 0.0 copy-start.5
  75.0 0.0 copy-start.2
  75.0 58.2 %all-gather.5.cloned.1.call-done = f32[512,512]{1,0:T(8,128)} async-done(((f32[32,512]{1,0:T(8,128)}), f32[512,512]{1,0:T(8,128)}) %all-gather.5.cloned.1.call-update) | async-done | bytes 1048592 | tf_op jit(solution)/shard_map/all_gather | solution.py:19
  133.2 2.8 broadcast_select_fusion.1
  136.0 0.0 copy-start.1
  136.0 0.0 copy-start.3
  136.0 0.0 all-reduce.3.cloned.1.call-update
  136.1 0.0 copy-done.4
  136.1 34.2 %all_gather.11 = f32[512,64]{1,0:T(8,128)S(1)} all-gather(f32[16,64]{1,0:T(8,128)S(1)} %copy-done.4), channel_id=1, replica_groups=mesh['row'=32,'col'=16] {'row'}, dimensions={0}, use_global_device_ids=true | all-gather | bytes 135168 | tf_op jit(solution)/shard_map/all_gather | solution.py:36
  170.3 0.0 copy-done.5
  170.3 0.0 copy-done.2
  170.3 1.8 fusion.13
  172.1 0.0 copy-done.1
  172.1 0.0 copy-done.3
  172.1 1.8 fusion.6
  174.0 179.8 %all-reduce.3.cloned.1.call-done = (f32[512,512]{1,0:T(8,128)}, f32[512,512]{1,0:T(8,128)}) async-done(((f32[512,512]{1,0:T(8,128)}, f32[512,512]{1,0:T(8,128)}), (f32[512,512]{1,0:T(8,128)}, f32[512,512]{1,0:T(8,128)})) %all-reduce.3.cloned.1.call-update) | async-done | bytes 2097168 | tf_op jit(solution)/shard_map/psum | solution.py:9
  353.7 6.7 %subtract_select_fusion = f32[512,1024]{1,0:T(8,128)} fusion(f32[512,1024]{1,0:T(8,128)} %param.6, f32[512,512]{1,0:T(8,128)S(1)} %copy-done.1, f32[512,512]{1,0:T(8,128)} %get-tuple-element.2, f32[512,512]{1,0:T(8,128)} %get-tuple-element.3, pred[1024]{0:T(1024)(128)(4,1)S(1)} %fusion.8), kind=kOutput, calls=%fused_computation | convolution fusion | flops 3222798336 | bytes 7341056 | tf_op jit(solution)/shard_map/dot_general | solution.py:30
  (2 shorter events, 0.0 us)
Async XLA Ops:
  7.2 65.2 %copy-start = (f32[32,512]{1,0:T(8,128)S(1)}, f32[32,512]{1,0:T(8,128)}, u32[]{:S(2)}) copy-start(f32[32,512]{1,0:T(8,128)} %param.7) | copy-start | bytes 196612
  7.2 65.1 %all-gather.3.cloned.1.call-start = ((), (), s32[]{:S(2)}) async-start(), calls=%async_computation | async-start | bytes 1114112 | tf_op jit(solution)/shard_map/all_gather | solution.py:15
  7.9 125.3 %all-gather.5.cloned.1.call-start = ((), (), s32[]{:S(2)}) async-start(), calls=%async_computation.1 | async-start | bytes 1114112 | tf_op jit(solution)/shard_map/all_gather | solution.py:19
  74.9 278.8 %all-reduce.3.cloned.1.call-start = ((), (), s32[]{:S(2)}) async-start(), calls=%async_computation.2 | async-start | bytes 4194304 | tf_op jit(solution)/shard_map/psum | solution.py:9
  75.0 61.1 %copy-start.4 = (f32[16,64]{1,0:T(8,128)S(1)}, f32[16,64]{1,0:T(8,128)}, u32[]{:S(2)}) copy-start(f32[16,64]{1,0:T(8,128)} %param.10) | copy-start | bytes 12292
  75.0 95.3 %copy-start.5 = (s32[64]{0:T(128)S(1)}, s32[64]{0:T(128)}, u32[]{:S(2)}) copy-start(s32[64]{0:T(128)} %param.11) | copy-start | bytes 772
  75.0 95.3 %copy-start.2 = (f32[512,512]{0,1:T(8,128)S(1)}, f32[512,512]{0,1:T(8,128)}, u32[]{:S(2)}) copy-start(f32[512,512]{0,1:T(8,128)} %all-gather.3.cloned.1.call-done) | copy-start | bytes 3145732
  136.0 36.1 %copy-start.1 = (f32[512,512]{1,0:T(8,128)S(1)}, f32[512,512]{1,0:T(8,128)}, u32[]{:S(2)}) copy-start(f32[512,512]{1,0:T(8,128)} %all-gather.5.cloned.1.call-done) | copy-start | bytes 3145732
  136.0 36.1 %copy-start.3 = (f32[512,64]{0,1:T(8,128)S(1)}, f32[512,64]{0,1:T(8,128)}, u32[]{:S(2)}) copy-start(f32[512,64]{0,1:T(8,128)} %param.9) | copy-start | bytes 393220
Sparse Core Ops, SparseCore 0:
  11.0 61.2 all-gather.2
  75.9 57.2 all-gather.4
  136.2 217.5 all-reduce.2
where the time goes:
time: 367 us
  waiting for transfers between devices  303 us (83%)
  blocking collectives  34.2 us (9%)
  between operations  13.8 us (4%)
  matrix products  12.9 us (4%)
    psum x1, waiting for transfers between devices, spread(): return lax.psum(jnp.where(mine, array, jnp.zeros_like(array)), axis)  180 us
    all_gather x1, waiting for transfers between devices, on_device(): inverse = lax.all_gather(inv_factor, 'col', axis=1, tiled=True)  64.4 us
    all_gather x1, waiting for transfers between devices, on_device(): row_block = lax.all_gather(solved_mine, 'col', axis=0, tiled=True)  58.2 us
    all_gather x1, blocking collectives, on_device(): fold_all = lax.all_gather(fold_series, 'row', axis=0, tiled=True)  34.2 us
  transfers between devices with their start and end apart: 3, of which 3 were waited for; matrix products, arithmetic and copies ran while one was open for 1% of the time, Pallas kernels for 0%

commit v1 on v0

--- a/solution.py
+++ b/solution.py
@@ -16,7 +16,14 @@
     solved_mine = lax.dot_general(
         panel, inverse, contract, precision=highest, preferred_element_type=jnp.float32
     )
-    row_block = lax.all_gather(solved_mine, "col", axis=0, tiled=True)
+    width = jax.lax.axis_size("col")
+    row_block = jax.lax.all_to_all(
+        jnp.tile(solved_mine, [width if jj == 0 else 1 for jj in range(solved_mine.ndim)]),
+        tiled=True,
+        concat_axis=0,
+        axis_name="col",
+        split_axis=0,
+    )
     rows_here = trailing.shape[0]
     cols_here = trailing.shape[1]
     tiles_across = cols_here // rows_here

time: 367 us -> 327 us (0.89)
  waiting for transfers between devices: 303 us -> 258 us
  starting transfers between devices: 0.12 us -> 4.45 us
    all_gather x1 -> x0, waiting for transfers between devices: 58.2 us -> none  [on_device(): row_block = lax.all_gather(solved_mine, 'col', axis=0, tiled=True)]
    all_to_all x0 -> x1, waiting for transfers between devices: none -> 14.2 us  [on_device(): jax.lax.all_to_all(jnp.tile(solved_mine, [width if jj == 0 else 1 for jj...]
    all_to_all x0 -> x1, starting transfers between devices: none -> 4.37 us  [on_device(): jax.lax.all_to_all(jnp.tile(solved_mine, [width if jj == 0 else 1 for jj...]
where the time goes in v1:
time: 327 us
  waiting for transfers between devices  258 us (79%)
  blocking collectives  35.5 us (11%)
  between operations  14.1 us (4%)
  matrix products  12.2 us (4%)
  starting transfers between devices  4.45 us (1%)
    psum x1, waiting for transfers between devices, spread(): return lax.psum(jnp.where(mine, array, jnp.zeros_like(array)), axis)  179 us
    all_gather x1, waiting for transfers between devices, on_device(): inverse = lax.all_gather(inv_factor, 'col', axis=1, tiled=True)  64.4 us
    all_gather x1, blocking collectives, on_device(): fold_all = lax.all_gather(fold_series, 'row', axis=0, tiled=True)  35.5 us
    all_to_all x1, waiting for transfers between devices, on_device(): jax.lax.all_to_all(jnp.tile(solved_mine, [width if jj == 0 else 1 for jj...  14.2 us
    dot_general x1, matrix products, on_device(): lax.dot_general(row_block, col_panel, contract, precision=highest, prefer...  6.69 us
  transfers between devices with their start and end apart: 3, of which 3 were waited for; matrix products, arithmetic and copies ran while one was open for 1% of the time, Pallas kernels for 0%

profile of v1, /device:TPU:1, one launch (start us, length us, event | category | flops | bytes accessed | tf_op | source)
XLA Modules:
  0.0 327.0 jit_solution(6694178178313173914)
XLA Ops:
  7.2 0.0 copy-start
  7.2 0.0 all-gather.2.cloned.1.call-start
  7.2 0.7 all-gather.2.cloned.1.call-update
  7.9 64.4 %all-gather.2.cloned.1.call-done = f32[512,512]{0,1:T(8,128)} async-done(((f32[512,32]{0,1:T(8,128)}), f32[512,512]{0,1:T(8,128)}) %all-gather.2.cloned.1.call-update) | async-done | bytes 1048592 | tf_op jit(solution)/shard_map/all_gather | solution.py:15
  72.3 0.0 copy-done
  72.3 1.9 fusion.12
  74.3 1.1 tile.2
  75.4 4.4 %all-to-all-start = ((f32[16,32,512]{2,1,0:T(8,128)}), f32[16,32,512]{2,1,0:T(8,128)S(1)}, u32[]{:S(2)}, u32[]{:S(2)}) async-start(f32[16,32,512]{2,1,0:T(8,128)} %tile.2), calls=%async_computation | async-start | bytes 2097152 | tf_op jit(solution)/shard_map/all_to_all | solution.py:20
  79.7 0.0 all-reduce.3.cloned.1.call-start
  79.8 0.0 copy-start.3
  79.8 0.0 copy-start.4
  79.8 0.0 copy-start.1
  79.8 14.2 %all-to-all-done = f32[16,32,512]{2,1,0:T(8,128)S(1)} async-done(((f32[16,32,512]{2,1,0:T(8,128)}), f32[16,32,512]{2,1,0:T(8,128)S(1)}, u32[]{:S(2)}, u32[]{:S(2)}) %all-to-all-start) | async-done | bytes 1048608 | tf_op jit(solution)/shard_map/all_to_all | solution.py:20
  94.0 1.6 broadcast_select_fusion.1
  95.6 0.0 copy-start.2
  95.6 0.0 all-reduce.3.cloned.1.call-update
  95.6 0.0 copy-done.3
  95.6 35.5 %all_gather.7 = f32[512,64]{1,0:T(8,128)S(1)} all-gather(f32[16,64]{1,0:T(8,128)S(1)} %copy-done.3), channel_id=1, replica_groups=mesh['row'=32,'col'=16] {'row'}, dimensions={0}, use_global_device_ids=true | all-gather | bytes 135168 | tf_op jit(solution)/shard_map/all_gather | solution.py:43
  131.2 0.0 copy-done.4
  131.2 0.0 copy-done.1
  131.2 1.8 fusion.13
  133.0 0.0 copy-done.2
  133.0 1.8 fusion.6
  134.8 178.6 %all-reduce.3.cloned.1.call-done = (f32[512,512]{1,0:T(8,128)}, f32[512,512]{1,0:T(8,128)}) async-done(((f32[512,512]{1,0:T(8,128)}, f32[512,512]{1,0:T(8,128)}), (f32[512,512]{1,0:T(8,128)}, f32[512,512]{1,0:T(8,128)})) %all-reduce.3.cloned.1.call-update) | async-done | bytes 2097168 | tf_op jit(solution)/shard_map/psum | solution.py:9
  313.4 6.7 %subtract_select_fusion = f32[512,1024]{1,0:T(8,128)} fusion(f32[512,1024]{1,0:T(8,128)} %param.6, f32[512,512]{1,0:T(8,128)S(1)} %bitcast.11, f32[512,512]{1,0:T(8,128)} %get-tuple-element.2, f32[512,512]{1,0:T(8,128)} %get-tuple-element.3, pred[1024]{0:T(1024)(128)(4,1)S(1)} %fusion.8), kind=kOutput, calls=%fused_computation | convolution fusion | flops 3222798336 | bytes 7341056 | tf_op jit(solution)/shard_map/dot_general | solution.py:37
  (2 shorter events, 0.0 us)
Async XLA Ops:
  7.2 65.2 %copy-start = (f32[32,512]{1,0:T(8,128)S(1)}, f32[32,512]{1,0:T(8,128)}, u32[]{:S(2)}) copy-start(f32[32,512]{1,0:T(8,128)} %param.7) | copy-start | bytes 196612
  7.2 65.1 %all-gather.2.cloned.1.call-start = ((), (), s32[]{:S(2)}) async-start(), calls=%async_computation.1 | async-start | bytes 1114112 | tf_op jit(solution)/shard_map/all_gather | solution.py:15
  75.4 18.7 %all-to-all-start = ((f32[16,32,512]{2,1,0:T(8,128)}), f32[16,32,512]{2,1,0:T(8,128)S(1)}, u32[]{:S(2)}, u32[]{:S(2)}) async-start(f32[16,32,512]{2,1,0:T(8,128)} %tile.2), calls=%async_computation | async-start | bytes 2097152 | tf_op jit(solution)/shard_map/all_to_all | solution.py:20
  79.7 233.7 %all-reduce.3.cloned.1.call-start = ((), (), s32[]{:S(2)}) async-start(), calls=%async_computation.2 | async-start | bytes 4194304 | tf_op jit(solution)/shard_map/psum | solution.py:9
  79.8 15.8 %copy-start.3 = (f32[16,64]{1,0:T(8,128)S(1)}, f32[16,64]{1,0:T(8,128)}, u32[]{:S(2)}) copy-start(f32[16,64]{1,0:T(8,128)} %param.10) | copy-start | bytes 12292
  79.8 51.3 %copy-start.4 = (s32[64]{0:T(128)S(1)}, s32[64]{0:T(128)}, u32[]{:S(2)}) copy-start(s32[64]{0:T(128)} %param.11) | copy-start | bytes 772
  79.8 51.4 %copy-start.1 = (f32[512,512]{0,1:T(8,128)S(1)}, f32[512,512]{0,1:T(8,128)}, u32[]{:S(2)}) copy-start(f32[512,512]{0,1:T(8,128)} %all-gather.2.cloned.1.call-done) | copy-start | bytes 3145732
  95.6 37.4 %copy-start.2 = (f32[512,64]{0,1:T(8,128)S(1)}, f32[512,64]{0,1:T(8,128)}, u32[]{:S(2)}) copy-start(f32[512,64]{0,1:T(8,128)} %param.9) | copy-start | bytes 393220
Sparse Core Ops, SparseCore 0:
  11.0 61.2 all-gather.1
  95.7 217.6 all-reduce.2
